TPU v7x, 32 devices: a whole 2x2x4 slice. The times are simulated.
32 devices in a mesh: dp: 8 (over z, x), seq: 4 (over y, core).
Axes of the slice: x: 2, y: 2, z: 4, core: 2. Of those that a mesh axis runs over, the one named last changes fastest.
Arguments:
- query_rows: bfloat16 [4096, 4096], P(('dp', 'seq')), may hold values from -60 to 60
- key_rows: bfloat16 [4096, 4096], P(('dp', 'seq')), may hold values from -5 to 5
- value_rows: bfloat16 [4096, 4096], P(('dp', 'seq')), may hold values from -12 to 12
- seg_ids: int32 [4096], P(('dp', 'seq')), may hold values from 0 to 15, as said below
- timesteps: int32 [16], replicated, may hold values from 0 to 999
- w_mod: bfloat16 [256, 4096], replicated, may hold values from -0.375 to 0.375
Outputs:
- mixed_rows: bfloat16 [4096, 4096], P(('dp', 'seq'))
Inputs may be any that keep to these rules, and one draw needn't show every extreme that they name: A row's bin is seg_ids // 2, a number below the size of dp. The 128 rows of one device hold at most 32 rows of any one bin, and for every index of seq some bin holds exactly 32 rows on each device of that index. Rows of one sample lie on many devices.
All inputs are finite; a program needn't handle non-finite values.
Results may differ from a plain program's by a relative error of at most 0.0058.
Values may be sent and summed in bfloat16 or wider, within the bound.
A program may use at most 128 MiB of HBM per device.

v0:
```python
import math

import jax
import jax.numpy as jnp
from jax import lax
from jax.sharding import PartitionSpec as P

HEAD_DIM = 128
FREQ = 256
SEG_BIN = 2


def for_sending(value):
    return jax.tree.map(lambda a: a.astype(jnp.bfloat16) if a.dtype == jnp.float32 else a, value)


def scale_rows_table(timesteps, w_mod):
    half_freq = FREQ // 2
    frequencies = jnp.exp(-math.log(10000.0) * jnp.arange(half_freq, dtype=jnp.float32) / half_freq)
    angles = timesteps.astype(jnp.float32)[:, None] * frequencies[None, :]
    embedding = jnp.concatenate([jnp.cos(angles), jnp.sin(angles)], axis=1)
    activated = jax.nn.silu(embedding).astype(jnp.bfloat16)
    return jnp.dot(activated, w_mod, preferred_element_type=jnp.float32)


def slot_places(row_bins, bin_count, capacity):
    bin_hits = (row_bins[:, None] == jnp.arange(bin_count, dtype=jnp.int32)[None, :]).astype(
        jnp.int32
    )
    ranks = jnp.cumsum(bin_hits, axis=0) - bin_hits
    slot_rank = jnp.sum(ranks * bin_hits, axis=1)
    target = row_bins * capacity + slot_rank
    return jnp.arange(bin_count * capacity, dtype=jnp.int32)[:, None] == target[None, :]


def slot_ids_of(placement, sample_ids):
    return jnp.sum(jnp.where(placement, sample_ids[None, :] + 1, 0), axis=1) - 1


def attend_slots(query_part, key_part, value_part, sample_ids):
    length, row_width = query_part.shape
    head_count = row_width // HEAD_DIM
    block_rows = min(512, length)
    score_scale = 1.0 / math.sqrt(HEAD_DIM)
    query_blocks = query_part.reshape(length // block_rows, block_rows, head_count, HEAD_DIM)
    key_heads = key_part.reshape(length, head_count, HEAD_DIM)
    value_heads = value_part.reshape(length, head_count, HEAD_DIM)
    id_blocks = sample_ids.reshape(length // block_rows, block_rows)

    def one_block(block_pair):
        query_block, query_ids = block_pair
        scores = (
            jnp.einsum("qhd,khd->hqk", query_block, key_heads, preferred_element_type=jnp.float32)
            * score_scale
        )
        same_sample = query_ids[:, None] == sample_ids[None, :]
        scores = jnp.where(same_sample[None], scores, -1e30)
        row_max = jnp.max(scores, axis=2, keepdims=True)
        weights = jnp.exp(scores - row_max)
        soft_probs = (weights / jnp.sum(weights, axis=2, keepdims=True)).astype(jnp.bfloat16)
        block_out = jnp.einsum(
            "hqk,khd->qhd", soft_probs, value_heads, preferred_element_type=jnp.float32
        )
        return block_out.astype(jnp.bfloat16).reshape(block_rows, row_width)

    return lax.map(one_block, (query_blocks, id_blocks)).reshape(length, row_width)


def place_rows(place_mask, arrays):
    return tuple(
        (
            jnp.dot(place_mask, single, preferred_element_type=jnp.float32).astype(jnp.bfloat16)
            for single in arrays
        )
    )


def shards(query_rows, key_rows, value_rows, seg_ids, timesteps, w_mod):
    dp_count = lax.axis_size("dp")
    seq_count = lax.axis_size("seq")
    row_count = query_rows.shape[0]
    capacity = 2 * row_count // dp_count
    ids_tiled = jnp.broadcast_to(seg_ids[:, None], (row_count, seq_count))
    group_ids = lax.all_to_all(ids_tiled, "seq", split_axis=1, concat_axis=0, tiled=True).reshape(
        -1
    )
    head_parts = (
        lax.all_to_all(query_rows, "seq", split_axis=1, concat_axis=0, tiled=True),
        lax.all_to_all(key_rows, "seq", split_axis=1, concat_axis=0, tiled=True),
        lax.all_to_all(value_rows, "seq", split_axis=1, concat_axis=0, tiled=True),
    )
    placement = slot_places(group_ids // SEG_BIN, dp_count, seq_count * capacity)
    place_mask = placement.astype(jnp.bfloat16)
    slotted = place_rows(place_mask, head_parts)
    bin_ids = lax.all_to_all(
        slot_ids_of(placement, group_ids), "dp", split_axis=0, concat_axis=0, tiled=True
    )
    bin_query, bin_key, bin_value = jax.tree.map(
        lambda part, own: part.astype(own.dtype),
        lax.all_to_all(for_sending(slotted), "dp", split_axis=0, concat_axis=0, tiled=True),
        slotted,
    )
    attended = attend_slots(bin_query, bin_key, bin_value, bin_ids)
    returned = lax.all_to_all(attended, "dp", split_axis=0, concat_axis=0, tiled=True)
    unslotted = jnp.dot(place_mask.T, returned, preferred_element_type=jnp.float32).astype(
        jnp.bfloat16
    )
    home_rows = lax.all_to_all(unslotted, "seq", split_axis=0, concat_axis=1, tiled=True)
    scale_table = scale_rows_table(timesteps, w_mod)
    lookup = (
        seg_ids[:, None] == jnp.arange(scale_table.shape[0], dtype=jnp.int32)[None, :]
    ).astype(jnp.float32)
    row_scales = jnp.dot(
        lookup, scale_table, precision=lax.Precision.HIGHEST, preferred_element_type=jnp.float32
    )
    return (home_rows.astype(jnp.float32) * (1.0 + row_scales)).astype(jnp.bfloat16)


def solution(mesh):
    placed = (
        P(("dp", "seq"), None),
        P(("dp", "seq"), None),
        P(("dp", "seq"), None),
        P(("dp", "seq")),
        P(),
        P(),
    )
    return jax.shard_map(
        shards, mesh=mesh, in_specs=placed, out_specs=P(("dp", "seq"), None), check_vma=False
    )
```

profile of v0, /device:TPU:9, one launch (start us, length us, event | category | flops | bytes accessed | tf_op | source)
XLA Modules:
  0.0 399.7 jit_solution(7302912907815652250)
XLA Ops:
  1.4 3.9 all-to-all-start
  5.3 3.0 all-to-all-done
  10.7 5.7 %all-to-all-start.1 = ((s32[8,128,1]{1,2,0:T(1,128)}), s32[8,128,1]{1,2,0:T(1,128)S(1)}, u32[]{:S(2)}, u32[]{:S(2)}) async-start(s32[8,128,1]{1,2,0:T(1,128)} %bitcast.11), calls=%async_computation.1 | async-start | bytes 8192 | tf_op jit(solution)/shard_map/all_to_all | solution.py:95
  20.4 5.8 %all-to-all-start.4 = ((bf16[128,4,1024]{0,2,1:T(8,128)(2,1)}), bf16[128,4,1024]{0,2,1:T(8,128)(2,1)S(1)}, u32[]{:S(2)}, u32[]{:S(2)}) async-start(bf16[128,4,1024]{0,2,1:T(8,128)(2,1)} %bitcast.79), calls=%async_computation.4 | async-start | bytes 2097152 | tf_op jit(solution)/shard_map/all_to_all | solution.py:89
  26.2 2.3 copy.40
  28.4 11.2 %all-to-all-done.4 = bf16[128,4,1024]{0,2,1:T(8,128)(2,1)S(1)} async-done(((bf16[128,4,1024]{0,2,1:T(8,128)(2,1)}), bf16[128,4,1024]{0,2,1:T(8,128)(2,1)S(1)}, u32[]{:S(2)}, u32[]{:S(2)}) %all-to-all-start.4) | async-done | bytes 1048608 | tf_op jit(solution)/shard_map/all_to_all | solution.py:89
  40.6 4.5 %all-to-all-start.6 = ((bf16[128,4,1024]{0,2,1:T(8,128)(2,1)}), bf16[128,4,1024]{0,2,1:T(8,128)(2,1)S(1)}, u32[]{:S(2)}, u32[]{:S(2)}) async-start(bf16[128,4,1024]{0,2,1:T(8,128)(2,1)} %bitcast.80), calls=%async_computation.6 | async-start | bytes 2097152 | tf_op jit(solution)/shard_map/all_to_all | solution.py:90
  47.3 11.2 %all-to-all-done.6 = bf16[128,4,1024]{0,2,1:T(8,128)(2,1)S(1)} async-done(((bf16[128,4,1024]{0,2,1:T(8,128)(2,1)}), bf16[128,4,1024]{0,2,1:T(8,128)(2,1)S(1)}, u32[]{:S(2)}, u32[]{:S(2)}) %all-to-all-start.6) | async-done | bytes 1048608 | tf_op jit(solution)/shard_map/all_to_all | solution.py:90
  59.5 4.5 %all-to-all-start.2 = ((bf16[128,4,1024]{0,2,1:T(8,128)(2,1)}), bf16[128,4,1024]{0,2,1:T(8,128)(2,1)S(1)}, u32[]{:S(2)}, u32[]{:S(2)}) async-start(bf16[128,4,1024]{0,2,1:T(8,128)(2,1)} %bitcast.78), calls=%async_computation.2 | async-start | bytes 2097152 | tf_op jit(solution)/shard_map/all_to_all | solution.py:88
  66.2 3.8 fusion.17
  70.1 7.4 %all-to-all-done.2 = bf16[128,4,1024]{0,2,1:T(8,128)(2,1)S(1)} async-done(((bf16[128,4,1024]{0,2,1:T(8,128)(2,1)}), bf16[128,4,1024]{0,2,1:T(8,128)(2,1)S(1)}, u32[]{:S(2)}, u32[]{:S(2)}) %all-to-all-start.2) | async-done | bytes 1048608 | tf_op jit(solution)/shard_map/all_to_all | solution.py:88
  77.4 5.4 %all-to-all-start.5 = ((bf16[8,128,1024]{2,1,0:T(8,128)(2,1)}), bf16[8,128,1024]{2,1,0:T(8,128)(2,1)}, u32[]{:S(2)}, u32[]{:S(2)}) async-start(bf16[8,128,1024]{2,1,0:T(8,128)(2,1)} %bitcast.83), calls=%async_computation.5 | async-start | bytes 4194304 | tf_op jit(solution)/shard_map/all_to_all | solution.py:100
  85.1 3.8 fusion.18
  88.9 40.5 %all-to-all-done.5 = bf16[8,128,1024]{2,1,0:T(8,128)(2,1)} async-done(((bf16[8,128,1024]{2,1,0:T(8,128)(2,1)}), bf16[8,128,1024]{2,1,0:T(8,128)(2,1)}, u32[]{:S(2)}, u32[]{:S(2)}) %all-to-all-start.5) | async-done | bytes 2097184 | tf_op jit(solution)/shard_map/all_to_all | solution.py:100
  129.4 5.6 %all-to-all-start.7 = ((bf16[8,128,1024]{2,1,0:T(8,128)(2,1)}), bf16[8,128,1024]{2,1,0:T(8,128)(2,1)}, u32[]{:S(2)}, u32[]{:S(2)}) async-start(bf16[8,128,1024]{2,1,0:T(8,128)(2,1)} %bitcast.84), calls=%async_computation.7 | async-start | bytes 4194304 | tf_op jit(solution)/shard_map/all_to_all | solution.py:100
  136.3 3.8 fusion.16
  140.1 41.4 %all-to-all-done.7 = bf16[8,128,1024]{2,1,0:T(8,128)(2,1)} async-done(((bf16[8,128,1024]{2,1,0:T(8,128)(2,1)}), bf16[8,128,1024]{2,1,0:T(8,128)(2,1)}, u32[]{:S(2)}, u32[]{:S(2)}) %all-to-all-start.7) | async-done | bytes 2097184 | tf_op jit(solution)/shard_map/all_to_all | solution.py:100
  181.5 5.7 %all-to-all-start.3 = ((bf16[8,128,1024]{2,1,0:T(8,128)(2,1)}), bf16[8,128,1024]{2,1,0:T(8,128)(2,1)}, u32[]{:S(2)}, u32[]{:S(2)}) async-start(bf16[8,128,1024]{2,1,0:T(8,128)(2,1)} %bitcast.82), calls=%async_computation.3 | async-start | bytes 4194304 | tf_op jit(solution)/shard_map/all_to_all | solution.py:100
  192.3 3.5 copy.54
  195.8 4.2 %copy.47 = bf16[1024,8,128]{0,2,1:T(8,128)(2,1)} copy(bf16[1024,8,128]{2,1,0:T(8,128)(2,1)} %bitcast.74) | data formatting | bytes 4194304 | tf_op jit(solution)/shard_map/reshape | solution.py:47
  199.9 33.5 %all-to-all-done.3 = bf16[8,128,1024]{2,1,0:T(8,128)(2,1)} async-done(((bf16[8,128,1024]{2,1,0:T(8,128)(2,1)}), bf16[8,128,1024]{2,1,0:T(8,128)(2,1)}, u32[]{:S(2)}, u32[]{:S(2)}) %all-to-all-start.3) | async-done | bytes 2097184 | tf_op jit(solution)/shard_map/all_to_all | solution.py:100
  233.5 3.5 copy.52
  237.0 85.8 %while.10 = (s32[]{:T(128)}, bf16[2,512,1024]{2,1,0:T(8,128)(2,1)}, s32[2,512]{1,0:T(2,128)S(1)}, s32[1024]{0:T(1024)S(1)}, bf16[2,512,8,128]{3,2,1,0:T(8,128)(2...) while((s32[]{:T(128)}, bf16[2,512,1024]{2,1,0:T(8,128)(2,1)}, ...), condition=%wide.region_7.8_spmd, body=%wide.region_4.7_spmd.sunk | while | flops 2182087680 | bytes 89172600 | solution.py:66
  238.9 8.1 %fusion.52 = f32[8,512,1024]{2,1,0:T(8,128)} fusion(bf16[1024,8,128]{2,0,1:T(8,128)(2,1)S(1)} %copy-done.1, bf16[1,512,8,128]{3,2,1,0:T(8,128)(2,1)S(1)} %constant_dynamic-slice_fusion.4), kind=kOutput, calls=%fused_computation.11.clone.1 | convolution fusion | flops 1073741824 | bytes 19922944 | tf_op jit(solution)/shard_map/while/body/eval_jaxpr/qhd,khd->hqk/dot_general | solution.py:53
  247.4 21.2 %fusion.53 = (f32[8,512]{1,0:T(8,128)S(1)}, f32[8,512,1024]{2,1,0:T(8,128)}) fusion(f32[8,512,1024]{2,1,0:T(8,128)} %fusion.52, pred[512,1024]{1,0:T(8,128)(4,1)S(1)} %broadcast_compare_fusion.2), kind=kOutput, calls=%fused_computation.71.clone.1 | output fusion | flops 25166848 | bytes 34095104 | tf_op jit(solution)/shard_map/while/body/eval_jaxpr/sub | solution.py:59
  268.6 8.8 %fusion.54 = bf16[8,512,128]{1,2,0:T(8,128)(2,1)} fusion(bf16[1024,8,128]{0,2,1:T(8,128)(2,1)} %get-tuple-element.160, f32[8,512,1024]{2,1,0:T(8,128)} %get-tuple-element.136, f32[8,512]{1,0:T(8,128)S(1)} %get-tuple-element.137), kind=kOutput, calls=%fused_computation.9.clone.1 | convolution fusion | flops 1082654720 | bytes 19939328 | tf_op jit(solution)/shard_map/while/body/eval_jaxpr/hqk,khd->qhd/dot_general | solution.py:61
  281.8 8.1 %fusion.52 = f32[8,512,1024]{2,1,0:T(8,128)} fusion(bf16[1024,8,128]{2,0,1:T(8,128)(2,1)S(1)} %copy-done.1, bf16[1,512,8,128]{3,2,1,0:T(8,128)(2,1)S(1)} %constant_dynamic-slice_fusion.4), kind=kOutput, calls=%fused_computation.11.clone.1 | convolution fusion | flops 1073741824 | bytes 19922944 | tf_op jit(solution)/shard_map/while/body/eval_jaxpr/qhd,khd->hqk/dot_general | solution.py:53
  290.3 21.2 %fusion.53 = (f32[8,512]{1,0:T(8,128)S(1)}, f32[8,512,1024]{2,1,0:T(8,128)}) fusion(f32[8,512,1024]{2,1,0:T(8,128)} %fusion.52, pred[512,1024]{1,0:T(8,128)(4,1)S(1)} %broadcast_compare_fusion.2), kind=kOutput, calls=%fused_computation.71.clone.1 | output fusion | flops 25166848 | bytes 34095104 | tf_op jit(solution)/shard_map/while/body/eval_jaxpr/sub | solution.py:59
  311.5 8.8 %fusion.54 = bf16[8,512,128]{1,2,0:T(8,128)(2,1)} fusion(bf16[1024,8,128]{0,2,1:T(8,128)(2,1)} %get-tuple-element.160, f32[8,512,1024]{2,1,0:T(8,128)} %get-tuple-element.136, f32[8,512]{1,0:T(8,128)S(1)} %get-tuple-element.137), kind=kOutput, calls=%fused_computation.9.clone.1 | convolution fusion | flops 1082654720 | bytes 19939328 | tf_op jit(solution)/shard_map/while/body/eval_jaxpr/hqk,khd->qhd/dot_general | solution.py:61
  322.8 52.4 %all_to_all.131 = bf16[8,128,1024]{2,1,0:T(8,128)(2,1)S(1)} all-to-all(bf16[8,128,1024]{2,1,0:T(8,128)(2,1)} %bitcast.81), channel_id=1, replica_groups=mesh['dp'=8,'seq'=4] {'dp'}, dimensions={0} | all-to-all | bytes 4194304 | tf_op jit(solution)/shard_map/all_to_all | solution.py:104
  377.6 5.7 %all-to-all-start.9 = ((bf16[4,128,1024]{2,1,0:T(8,128)(2,1)}), bf16[4,128,1024]{2,1,0:T(8,128)(2,1)S(1)}, u32[]{:S(2)}, u32[]{:S(2)}) async-start(bf16[4,128,1024]{2,1,0:T(8,128)(2,1)} %bitcast.86), calls=%async_computation.9 | async-start | bytes 2097152 | tf_op jit(solution)/shard_map/all_to_all | solution.py:108
  383.8 12.9 %all-to-all-done.9 = bf16[4,128,1024]{2,1,0:T(8,128)(2,1)S(1)} async-done(((bf16[4,128,1024]{2,1,0:T(8,128)(2,1)}), bf16[4,128,1024]{2,1,0:T(8,128)(2,1)S(1)}, u32[]{:S(2)}, u32[]{:S(2)}) %all-to-all-start.9) | async-done | bytes 1048608 | tf_op jit(solution)/shard_map/all_to_all | solution.py:108
  (60 shorter events, 38.4 us)
Async XLA Ops:
  0.0 383.4 %copy-start = (bf16[256,4096]{1,0:T(8,128)(2,1)S(1)}, bf16[256,4096]{1,0:T(8,128)(2,1)}, u32[]{:S(2)}) copy-start(bf16[256,4096]{1,0:T(8,128)(2,1)} %param.13) | copy-start | bytes 6291460
  1.4 6.9 %all-to-all-start = ((s32[128,4,1]{0,2,1:T(1,128)}), s32[128,4,1]{0,2,1:T(1,128)S(1)}, u32[]{:S(2)}, u32[]{:S(2)}) async-start(s32[128,4,1]{0,2,1:T(1,128)} %broadcast_in_dim.37), calls=%async_computation | async-start | bytes 4096 | tf_op jit(solution)/shard_map/all_to_all | solution.py:84
  9.8 126.5 %copy-start.4 = (s32[512]{0:T(512)}, s32[512]{0:T(512)S(1)}, u32[]{:S(2)}) copy-start(s32[512]{0:T(512)S(1)} %multiply_add_fusion) | copy-start | bytes 6148
  10.7 9.7 %all-to-all-start.1 = ((s32[8,128,1]{1,2,0:T(1,128)}), s32[8,128,1]{1,2,0:T(1,128)S(1)}, u32[]{:S(2)}, u32[]{:S(2)}) async-start(s32[8,128,1]{1,2,0:T(1,128)} %bitcast.11), calls=%async_computation.1 | async-start | bytes 8192 | tf_op jit(solution)/shard_map/all_to_all | solution.py:95
  20.4 19.2 %all-to-all-start.4 = ((bf16[128,4,1024]{0,2,1:T(8,128)(2,1)}), bf16[128,4,1024]{0,2,1:T(8,128)(2,1)S(1)}, u32[]{:S(2)}, u32[]{:S(2)}) async-start(bf16[128,4,1024]{0,2,1:T(8,128)(2,1)} %bitcast.79), calls=%async_computation.4 | async-start | bytes 2097152 | tf_op jit(solution)/shard_map/all_to_all | solution.py:89
  39.6 1.0 copy-start.3
  40.6 17.9 %all-to-all-start.6 = ((bf16[128,4,1024]{0,2,1:T(8,128)(2,1)}), bf16[128,4,1024]{0,2,1:T(8,128)(2,1)S(1)}, u32[]{:S(2)}, u32[]{:S(2)}) async-start(bf16[128,4,1024]{0,2,1:T(8,128)(2,1)} %bitcast.80), calls=%async_computation.6 | async-start | bytes 2097152 | tf_op jit(solution)/shard_map/all_to_all | solution.py:90
  58.5 1.0 copy-start.2
  59.5 17.9 %all-to-all-start.2 = ((bf16[128,4,1024]{0,2,1:T(8,128)(2,1)}), bf16[128,4,1024]{0,2,1:T(8,128)(2,1)S(1)}, u32[]{:S(2)}, u32[]{:S(2)}) async-start(bf16[128,4,1024]{0,2,1:T(8,128)(2,1)} %bitcast.78), calls=%async_computation.2 | async-start | bytes 2097152 | tf_op jit(solution)/shard_map/all_to_all | solution.py:88
  77.4 52.0 %all-to-all-start.5 = ((bf16[8,128,1024]{2,1,0:T(8,128)(2,1)}), bf16[8,128,1024]{2,1,0:T(8,128)(2,1)}, u32[]{:S(2)}, u32[]{:S(2)}) async-start(bf16[8,128,1024]{2,1,0:T(8,128)(2,1)} %bitcast.83), calls=%async_computation.5 | async-start | bytes 4194304 | tf_op jit(solution)/shard_map/all_to_all | solution.py:100
  129.4 52.1 %all-to-all-start.7 = ((bf16[8,128,1024]{2,1,0:T(8,128)(2,1)}), bf16[8,128,1024]{2,1,0:T(8,128)(2,1)}, u32[]{:S(2)}, u32[]{:S(2)}) async-start(bf16[8,128,1024]{2,1,0:T(8,128)(2,1)} %bitcast.84), calls=%async_computation.7 | async-start | bytes 4194304 | tf_op jit(solution)/shard_map/all_to_all | solution.py:100
  181.5 52.0 %all-to-all-start.3 = ((bf16[8,128,1024]{2,1,0:T(8,128)(2,1)}), bf16[8,128,1024]{2,1,0:T(8,128)(2,1)}, u32[]{:S(2)}, u32[]{:S(2)}) async-start(bf16[8,128,1024]{2,1,0:T(8,128)(2,1)} %bitcast.82), calls=%async_computation.3 | async-start | bytes 4194304 | tf_op jit(solution)/shard_map/all_to_all | solution.py:100
  237.0 1.9 copy-start.1
  279.9 1.9 copy-start.1
  322.8 52.4 %copy-start.5 = (s32[512]{0:T(512)S(1)}, s32[512]{0:T(512)}, u32[]{:S(2)}) copy-start(s32[512]{0:T(512)} %copy-done.4) | copy-start | bytes 6148
  377.6 5.7 %copy-start.7 = (s32[16]{0:T(128)S(1)}, s32[16]{0:T(128)}, u32[]{:S(2)}) copy-start(s32[16]{0:T(128)} %param.12) | copy-start | bytes 196
  377.6 19.1 %all-to-all-start.9 = ((bf16[4,128,1024]{2,1,0:T(8,128)(2,1)}), bf16[4,128,1024]{2,1,0:T(8,128)(2,1)S(1)}, u32[]{:S(2)}, u32[]{:S(2)}) async-start(bf16[4,128,1024]{2,1,0:T(8,128)(2,1)} %bitcast.86), calls=%async_computation.9 | async-start | bytes 2097152 | tf_op jit(solution)/shard_map/all_to_all | solution.py:108
  397.0 0.7 copy-start.6
where the time goes:
time: 403 us; the launch traced here: 400 us
  waiting for transfers between devices  163 us (40%)
  blocking collectives  52.4 us (13%)
  matrix products  49.9 us (12%)
  starting transfers between devices  46.6 us (12%)
  other arithmetic  46.4 us (12%)
  local copies, waits for them, and re-layouts  41.4 us (10%)
    all_to_all x3, waiting for transfers between devices, shards(): lax.all_to_all(for_sending(slotted), 'dp', split_axis=0, concat_axis=0, t...  115 us
    all_to_all x1, blocking collectives, shards(): lax.all_to_all(attended, 'dp', split_axis=0, concat_axis=0, tiled=True)  52.4 us
    sub x2, other arithmetic, one_block(): weights = jnp.exp(scores - row_max)  42.4 us
    unnamed x20, local copies, waits for them, and re-layouts  18.4 us
    dot_general x2, matrix products, one_block(): jnp.einsum('hqk,khd->qhd', soft_probs, value_heads, preferred_element_typ...  17.5 us
    all_to_all x3, starting transfers between devices, shards(): lax.all_to_all(for_sending(slotted), 'dp', split_axis=0, concat_axis=0, t...  16.7 us
    dot_general x2, matrix products, one_block(): jnp.einsum('qhd,khd->hqk', query_block, key_heads, preferred_element_type...  16.2 us
    all_to_all x1, waiting for transfers between devices, shards(): lax.all_to_all(unslotted, 'seq', split_axis=0, concat_axis=1, tiled=True)  12.9 us
  transfers between devices with their start and end apart: 9, of which 9 were waited for; matrix products, arithmetic and copies ran while one was open for 9% of the time, Pallas kernels for 0%

commit v1 on v0

--- a/solution.py
+++ b/solution.py
@@ -1,8 +1,11 @@
+import functools
 import math
 
 import jax
 import jax.numpy as jnp
 from jax import lax
+from jax.experimental import pallas as pl
+from jax.experimental.pallas import tpu as pltpu
 from jax.sharding import PartitionSpec as P
 
 HEAD_DIM = 128
@@ -75,7 +78,7 @@
     )
 
 
-def shards(query_rows, key_rows, value_rows, seg_ids, timesteps, w_mod):
+def routed_shards(query_rows, key_rows, value_rows, seg_ids, timesteps, w_mod):
     dp_count = lax.axis_size("dp")
     seq_count = lax.axis_size("seq")
     row_count = query_rows.shape[0]
@@ -114,6 +117,295 @@
         lookup, scale_table, precision=lax.Precision.HIGHEST, preferred_element_type=jnp.float32
     )
     return (home_rows.astype(jnp.float32) * (1.0 + row_scales)).astype(jnp.bfloat16)
+
+
+EXCLUDED = float(1 << 20)
+NT = (((1,), (1,)), ((), ()))
+TN = (((0,), (0,)), ((), ()))
+
+
+def head_kernel(
+    sizes,
+    q_ref,
+    k_ref,
+    v_ref,
+    ids_ref,
+    table_ref,
+    out_ref,
+    rows_buf,
+    ids_buf,
+    place_buf,
+    q_slots,
+    k_slots,
+    v_slots,
+    group_out,
+    out_buf,
+    sem_send,
+    sem_recv,
+    sem_out_send,
+    sem_out_recv,
+):
+    dp_count, seq_count, capacity, group = sizes
+    count = dp_count * seq_count
+    row_count = q_ref.shape[0]
+    slot_count = dp_count * capacity
+    me = lax.axis_index("dp") * seq_count + lax.axis_index("seq")
+    sources = (k_ref, q_ref, v_ref)
+
+    def device_of(index):
+        return (index // seq_count, index % seq_count)
+
+    def head_columns(index):
+        return pl.ds(pl.multiple_of(index * HEAD_DIM, HEAD_DIM), HEAD_DIM)
+
+    def part_copy(part, target, origin):
+        return pltpu.make_async_remote_copy(
+            src_ref=sources[part].at[:, head_columns(target)],
+            dst_ref=rows_buf.at[origin, :, pl.ds(part * HEAD_DIM, HEAD_DIM)],
+            send_sem=sem_send.at[part, target],
+            recv_sem=sem_recv.at[part, origin],
+            device_id=device_of(target),
+            device_id_type=pl.DeviceIdType.MESH,
+        )
+
+    def ids_copy(target, origin):
+        return pltpu.make_async_remote_copy(
+            src_ref=ids_ref,
+            dst_ref=ids_buf.at[origin],
+            send_sem=sem_send.at[3, target],
+            recv_sem=sem_recv.at[3, origin],
+            device_id=device_of(target),
+            device_id_type=pl.DeviceIdType.MESH,
+        )
+
+    def own_copy(part):
+        return pltpu.make_async_copy(
+            sources[part].at[:, head_columns(me)],
+            rows_buf.at[me, :, pl.ds(part * HEAD_DIM, HEAD_DIM)],
+            sem_recv.at[part, me],
+        )
+
+    def out_copy(target, origin):
+        return pltpu.make_async_remote_copy(
+            src_ref=out_buf.at[target],
+            dst_ref=out_ref.at[:, head_columns(origin)],
+            send_sem=sem_out_send.at[target],
+            recv_sem=sem_out_recv.at[origin],
+            device_id=device_of(target),
+            device_id_type=pl.DeviceIdType.MESH,
+        )
+
+    def own_out():
+        return pltpu.make_async_copy(
+            out_buf.at[me], out_ref.at[:, head_columns(me)], sem_out_send.at[me]
+        )
+
+    for part in range(3):
+        own_copy(part).start()
+
+    barrier = pltpu.get_barrier_semaphore()
+
+    @pl.loop(1, count)
+    def _(step):
+        pl.semaphore_signal(
+            barrier,
+            inc=1,
+            device_id=device_of((me + step) % count),
+            device_id_type=pl.DeviceIdType.MESH,
+        )
+
+    pl.semaphore_wait(barrier, count - 1)
+
+    @pl.loop(1, count)
+    def _(step):
+        ids_copy((me + step) % count, me).start()
+
+    @pl.loop(1, count)
+    def _(step):
+        part_copy(0, (me + step) % count, me).start()
+        part_copy(1, (me + step) % count, me).start()
+
+    @pl.loop(1, count)
+    def _(step):
+        part_copy(2, (me + step) % count, me).start()
+
+    v_slots[:, :, HEAD_DIM:] = jnp.ones(
+        (dp_count, count * capacity, HEAD_DIM), jnp.bfloat16
+    )
+    before = (
+        lax.broadcasted_iota(jnp.int32, (row_count, row_count), 0)
+        < lax.broadcasted_iota(jnp.int32, (row_count, row_count), 1)
+    ).astype(jnp.bfloat16)
+    part_lane = lax.broadcasted_iota(jnp.int32, (1, HEAD_DIM), 1) < SEG_BIN
+
+    def place_qk(origin, ids):
+        ids_row = ids[0:1, :]
+        bins = ids_row // SEG_BIN
+        member = ids_row - bins * SEG_BIN
+        bin_hits = lax.broadcasted_iota(jnp.int32, (16, row_count), 0) == bins
+        ranks = jnp.dot(
+            bin_hits.astype(jnp.bfloat16), before, preferred_element_type=jnp.float32
+        )
+        rank = jnp.sum(jnp.where(bin_hits, ranks, 0.0), axis=0, keepdims=True)
+        slot = bins * capacity + rank.astype(jnp.int32)
+        place = (
+            lax.broadcasted_iota(jnp.int32, (slot_count, row_count), 0) == slot
+        ).astype(jnp.bfloat16)
+        place_buf[origin] = place
+        member_hits = (
+            lax.broadcasted_iota(jnp.int32, (HEAD_DIM, row_count), 0) == member
+        )
+        own_member = lax.dot_general(
+            place, member_hits.astype(jnp.bfloat16), NT, preferred_element_type=jnp.float32
+        )
+        other_member = lax.dot_general(
+            place,
+            jnp.logical_not(member_hits).astype(jnp.bfloat16),
+            NT,
+            preferred_element_type=jnp.float32,
+        )
+        q_marks = jnp.where(part_lane, (own_member - 1.0) * EXCLUDED, 0.0)
+        k_marks = jnp.where(part_lane, 1.0 - other_member, 0.0)
+        placed = jnp.dot(
+            place, rows_buf[origin, :, : 2 * HEAD_DIM], preferred_element_type=jnp.float32
+        ).astype(jnp.bfloat16)
+        at = pl.ds(pl.multiple_of(origin * capacity, capacity), capacity)
+        shape = (dp_count, capacity, HEAD_DIM)
+        k_slots[:, at, :HEAD_DIM] = placed[:, :HEAD_DIM].reshape(shape)
+        q_slots[:, at, :HEAD_DIM] = placed[:, HEAD_DIM:].reshape(shape)
+        k_slots[:, at, HEAD_DIM:] = k_marks.astype(jnp.bfloat16).reshape(shape)
+        q_slots[:, at, HEAD_DIM:] = q_marks.astype(jnp.bfloat16).reshape(shape)
+
+    def place_v(origin):
+        placed = jnp.dot(
+            place_buf[origin],
+            rows_buf[origin, :, 2 * HEAD_DIM :],
+            preferred_element_type=jnp.float32,
+        ).astype(jnp.bfloat16)
+        at = pl.ds(pl.multiple_of(origin * capacity, capacity), capacity)
+        v_slots[:, at, :HEAD_DIM] = placed.reshape((dp_count, capacity, HEAD_DIM))
+
+    own_copy(0).wait()
+    own_copy(1).wait()
+    place_qk(me, ids_ref[...])
+
+    @pl.loop(1, count)
+    def _(step):
+        origin = (me - step + count) % count
+        ids_copy(me, origin).wait_recv()
+        part_copy(0, me, origin).wait_recv()
+        part_copy(1, me, origin).wait_recv()
+        place_qk(origin, ids_buf[origin])
+
+    own_copy(2).wait()
+    place_v(me)
+
+    @pl.loop(1, count)
+    def _(step):
+        origin = (me - step + count) % count
+        part_copy(2, me, origin).wait_recv()
+        place_v(origin)
+
+    exponent_scale = 1.0 / (math.sqrt(HEAD_DIM) * math.log(2.0))
+    group_slots = group * capacity
+
+    @pl.loop(0, count // group)
+    def _(turn):
+        first = ((me // group + turn + 1) % (count // group)) * group
+        at = pl.ds(pl.multiple_of(first * capacity, group_slots), group_slots)
+
+        @pl.loop(0, dp_count)
+        def _(bin_index):
+            query = q_slots[bin_index, at, :]
+            scores = lax.dot_general(
+                query, k_slots[bin_index], NT, preferred_element_type=jnp.float32
+            )
+            row_max = jnp.max(scores, axis=1, keepdims=True)
+            weights = jnp.exp2((scores - row_max) * exponent_scale).astype(jnp.bfloat16)
+            sums = jnp.dot(weights, v_slots[bin_index], preferred_element_type=jnp.float32)
+            attended = (sums[:, :HEAD_DIM] / sums[:, HEAD_DIM:]).astype(jnp.bfloat16)
+            factor = jnp.zeros((group_slots, HEAD_DIM), jnp.float32)
+            for member in range(SEG_BIN):
+                mark = query[:, HEAD_DIM + member : HEAD_DIM + member + 1].astype(jnp.float32)
+                row = table_ref[pl.ds(bin_index * SEG_BIN + member, 1), :]
+                factor = jnp.where(mark == 0.0, 1.0 + row, factor)
+            mixed = (attended.astype(jnp.float32) * factor).astype(jnp.bfloat16)
+            group_out[bin_index] = mixed
+
+        for inner in range(group):
+            target = first + inner
+            slots = group_out[:, inner * capacity : (inner + 1) * capacity, :].reshape(
+                (slot_count, HEAD_DIM)
+            )
+            out_buf[target] = lax.dot_general(
+                place_buf[target], slots, TN, preferred_element_type=jnp.float32
+            ).astype(jnp.bfloat16)
+
+            @pl.when(target != me)
+            def _():
+                out_copy(target, me).start()
+
+            @pl.when(target == me)
+            def _():
+                own_out().start()
+
+    @pl.loop(1, count)
+    def _(step):
+        target = (me + step) % count
+        ids_copy(target, me).wait_send()
+        part_copy(0, target, me).wait_send()
+        part_copy(1, target, me).wait_send()
+        part_copy(2, target, me).wait_send()
+        out_copy(target, me).wait_send()
+        out_copy(me, target).wait_recv()
+
+    own_out().wait()
+
+
+def head_shards(query_rows, key_rows, value_rows, seg_ids, timesteps, w_mod):
+    dp_count = lax.axis_size("dp")
+    seq_count = lax.axis_size("seq")
+    count = dp_count * seq_count
+    row_count, width = query_rows.shape
+    capacity = 2 * row_count // dp_count
+    group = min(8, count)
+    me = lax.axis_index("dp") * seq_count + lax.axis_index("seq")
+    head_weights = lax.dynamic_slice_in_dim(w_mod, me * HEAD_DIM, HEAD_DIM, 1)
+    scale_table = scale_rows_table(timesteps, head_weights)
+    ids = jnp.broadcast_to(seg_ids[None, :], (8, row_count))
+    vmem = pl.BlockSpec(memory_space=pltpu.VMEM)
+    anywhere = pl.BlockSpec(memory_space=pl.ANY)
+    slots = (dp_count, count * capacity, 2 * HEAD_DIM)
+    return pl.pallas_call(
+        functools.partial(head_kernel, (dp_count, seq_count, capacity, group)),
+        out_shape=jax.ShapeDtypeStruct((row_count, width), jnp.bfloat16),
+        in_specs=[anywhere, anywhere, anywhere, vmem, vmem],
+        out_specs=anywhere,
+        scratch_shapes=[
+            pltpu.VMEM((count, row_count, 3 * HEAD_DIM), jnp.bfloat16),
+            pltpu.VMEM((count, 8, row_count), jnp.int32),
+            pltpu.VMEM((count, dp_count * capacity, row_count), jnp.bfloat16),
+            pltpu.VMEM(slots, jnp.bfloat16),
+            pltpu.VMEM(slots, jnp.bfloat16),
+            pltpu.VMEM(slots, jnp.bfloat16),
+            pltpu.VMEM((dp_count, group * capacity, HEAD_DIM), jnp.bfloat16),
+            pltpu.VMEM((count, row_count, HEAD_DIM), jnp.bfloat16),
+            pltpu.SemaphoreType.DMA((4, count)),
+            pltpu.SemaphoreType.DMA((4, count)),
+            pltpu.SemaphoreType.DMA((count,)),
+            pltpu.SemaphoreType.DMA((count,)),
+        ],
+        compiler_params=pltpu.CompilerParams(
+            collective_id=0, has_side_effects=True, vmem_limit_bytes=56 * 1024 * 1024
+        ),
+    )(query_rows, key_rows, value_rows, ids, scale_table)
+
+
+def shards(query_rows, key_rows, value_rows, seg_ids, timesteps, w_mod):
+    count = lax.axis_size("dp") * lax.axis_size("seq")
+    whole_heads = query_rows.shape[1] == count * HEAD_DIM
+    body = head_shards if whole_heads else routed_shards
+    return body(query_rows, key_rows, value_rows, seg_ids, timesteps, w_mod)
 
 
 def solution(mesh):

time: 403 us -> 131 us (0.33)
  waiting for transfers between devices: 163 us -> 0 us
  Pallas kernels: 0 us -> 126 us
  blocking collectives: 52.4 us -> 0 us
  matrix products: 49.9 us -> 0.74 us
  starting transfers between devices: 46.6 us -> 0 us
  other arithmetic: 46.4 us -> 0.93 us
  local copies, waits for them, and re-layouts: 41.4 us -> 3.54 us
    all_to_all x9 -> x0, waiting for transfers between devices: 163 us -> none  [the longest x3 115 us: shards(): lax.all_to_all(for_sending(slotted), 'dp', split_axis=0, concat_axis=0, t...]
    pallas_call x0 -> x1, Pallas kernels: none -> 126 us  [head_shards(): pl.pallas_call(functools.partial(head_kernel, (dp_count, seq_count, capac...]
    all_to_all x1 -> x0, blocking collectives: 52.4 us -> none  [shards(): lax.all_to_all(attended, 'dp', split_axis=0, concat_axis=0, tiled=True)]
    dot_general x9 -> x0, matrix products: 49.5 us -> none  [the longest x2 17.5 us: one_block(): jnp.einsum('hqk,khd->qhd', soft_probs, value_heads, preferred_element_typ...]
    all_to_all x9 -> x0, starting transfers between devices: 46.6 us -> none  [the longest x3 16.7 us: shards(): lax.all_to_all(for_sending(slotted), 'dp', split_axis=0, concat_axis=0, t...]
    sub x3 -> x0, other arithmetic: 43 us -> none  [the longest x2 42.4 us: one_block(): weights = jnp.exp(scores - row_max)]
    unnamed x20 -> x3, local copies, waits for them, and re-layouts: 18.4 us -> 2.29 us
    all_to_all x4 -> x0, local copies, waits for them, and re-layouts: 6.35 us -> none  [the longest x1 2.28 us: shards(): lax.all_to_all(key_rows, 'seq', split_axis=1, concat_axis=0, tiled=True)]
  transfers between devices with their start and end apart: 9 -> 0, of which waited for: 9 -> 0; matrix products, arithmetic and copies ran while one was open for 9% -> 0% of each run, Pallas kernels for 0% -> 0%
where the time goes in v1:
time: 131 us
  Pallas kernels  126 us (96%)
  local copies, waits for them, and re-layouts  3.54 us (3%)
    pallas_call x1, Pallas kernels, head_shards(): pl.pallas_call(functools.partial(head_kernel, (dp_count, seq_count, capac...  126 us

profile of v1, /device:TPU:9, one launch (start us, length us, event | category | flops | bytes accessed | tf_op | source)
XLA Modules:
  0.0 130.8 jit_solution(6799024455389609735)
XLA Ops:
  0.0 0.0 copy-start
  0.0 0.8 convert_element_type.6
  0.8 1.2 broadcast_in_dim.2.ids_ref
  2.1 0.1 multiply_cosine_fusion
  2.2 0.0 copy-done
  2.2 0.7 fusion.table_ref
  2.9 125.5 %shard_map.64 = bf16[128,4096]{1,0:T(8,128)(2,1)} custom-call(bf16[128,4096]{1,0:T(8,128)(2,1)} %q_ref.1, bf16[128,4096]{1,0:T(8,128)(2,1)} %k_ref.1, bf16[128,4096]{1,0:T(8,128)(2,1)} %v_ref.1, s32[8,128]{1,0:T(8,128)} %broadcast_in_dim.2.ids_ref, f32[16,128]{1,0:T(8,128)} %fusion.table_ref), custom_call_target="tpu_custom_call" | custom-call | tf_op jit(solution)/shard_map/pallas_call | solution.py:379
  128.5 2.3 %copy.8 = bf16[128,4096]{1,0:T(8,128)(2,1)} copy(bf16[128,4096]{1,0:T(8,128)(2,1)} %shard_map.64) | data formatting | bytes 2097152
  (1 shorter events, 0.0 us)
Async XLA Ops:
  0.0 2.2 %copy-start = (bf16[256,4096]{1,0:T(8,128)(2,1)S(1)}, bf16[256,4096]{1,0:T(8,128)(2,1)}, u32[]{:S(2)}) copy-start(bf16[256,4096]{1,0:T(8,128)(2,1)} %param.11) | copy-start | bytes 6291460

commit v2 on v1

--- a/solution.py
+++ b/solution.py
@@ -138,6 +138,7 @@
     q_slots,
     k_slots,
     v_slots,
+    weights_buf,
     group_out,
     out_buf,
     sem_send,
@@ -155,6 +156,20 @@
     def device_of(index):
         return (index // seq_count, index % seq_count)
 
+    half = count // 2
+
+    def peer(away, shift):
+        return ((me // half + away) % 2) * half + (me % half + shift + half) % half
+
+    def each_peer(visit):
+        @pl.loop(0, half)
+        def _(shift):
+            visit(1, shift)
+
+            @pl.when(shift > 0)
+            def _():
+                visit(0, shift)
+
     def head_columns(index):
         return pl.ds(pl.multiple_of(index * HEAD_DIM, HEAD_DIM), HEAD_DIM)
 
@@ -205,29 +220,25 @@
 
     barrier = pltpu.get_barrier_semaphore()
 
-    @pl.loop(1, count)
-    def _(step):
+    def greet(away, shift):
         pl.semaphore_signal(
             barrier,
             inc=1,
-            device_id=device_of((me + step) % count),
+            device_id=device_of(peer(away, shift)),
             device_id_type=pl.DeviceIdType.MESH,
         )
 
+    each_peer(greet)
     pl.semaphore_wait(barrier, count - 1)
 
-    @pl.loop(1, count)
-    def _(step):
-        ids_copy((me + step) % count, me).start()
-
-    @pl.loop(1, count)
-    def _(step):
-        part_copy(0, (me + step) % count, me).start()
-        part_copy(1, (me + step) % count, me).start()
-
-    @pl.loop(1, count)
-    def _(step):
-        part_copy(2, (me + step) % count, me).start()
+    def send_qk(away, shift):
+        target = peer(away, shift)
+        ids_copy(target, me).start()
+        part_copy(0, target, me).start()
+        part_copy(1, target, me).start()
+
+    each_peer(send_qk)
+    each_peer(lambda away, shift: part_copy(2, peer(away, shift), me).start())
 
     v_slots[:, :, HEAD_DIM:] = jnp.ones(
         (dp_count, count * capacity, HEAD_DIM), jnp.bfloat16
@@ -239,9 +250,8 @@
     part_lane = lax.broadcasted_iota(jnp.int32, (1, HEAD_DIM), 1) < SEG_BIN
 
     def place_qk(origin, ids):
-        ids_row = ids[0:1, :]
-        bins = ids_row // SEG_BIN
-        member = ids_row - bins * SEG_BIN
+        bins = ids // SEG_BIN
+        member = ids - bins * SEG_BIN
         bin_hits = lax.broadcasted_iota(jnp.int32, (16, row_count), 0) == bins
         ranks = jnp.dot(
             bin_hits.astype(jnp.bfloat16), before, preferred_element_type=jnp.float32
@@ -289,44 +299,71 @@
     own_copy(1).wait()
     place_qk(me, ids_ref[...])
 
-    @pl.loop(1, count)
-    def _(step):
-        origin = (me - step + count) % count
+    def take_qk(away, shift):
+        origin = peer(away, -shift)
         ids_copy(me, origin).wait_recv()
         part_copy(0, me, origin).wait_recv()
         part_copy(1, me, origin).wait_recv()
         place_qk(origin, ids_buf[origin])
 
+    each_peer(take_qk)
+
+    exponent_scale = 1.0 / (math.sqrt(HEAD_DIM) * math.log(2.0))
+    group_slots = group * capacity
+    groups = count // group
+
+    def group_at(turn):
+        first = ((me // group + groups // 2 + turn) % groups) * group
+        return first, pl.ds(pl.multiple_of(first * capacity, group_slots), group_slots)
+
+    @pl.loop(0, groups)
+    def _(turn):
+        _, at = group_at(turn)
+
+        @pl.loop(0, dp_count)
+        def _(bin_index):
+            scores = lax.dot_general(
+                q_slots[bin_index, at, :],
+                k_slots[bin_index],
+                NT,
+                preferred_element_type=jnp.float32,
+            )
+            row_max = jnp.max(scores, axis=1, keepdims=True)
+            weights_buf[bin_index, at, :] = jnp.exp2(
+                (scores - row_max) * exponent_scale
+            ).astype(jnp.bfloat16)
+
     own_copy(2).wait()
     place_v(me)
 
-    @pl.loop(1, count)
-    def _(step):
-        origin = (me - step + count) % count
+    @pl.loop(1, half)
+    def _(shift):
+        origin = peer(0, -shift)
         part_copy(2, me, origin).wait_recv()
         place_v(origin)
 
-    exponent_scale = 1.0 / (math.sqrt(HEAD_DIM) * math.log(2.0))
-    group_slots = group * capacity
-
-    @pl.loop(0, count // group)
+    @pl.loop(0, half)
+    def _(shift):
+        origin = peer(1, -shift)
+        part_copy(2, me, origin).wait_recv()
+        place_v(origin)
+
+    @pl.loop(0, groups)
     def _(turn):
-        first = ((me // group + turn + 1) % (count // group)) * group
-        at = pl.ds(pl.multiple_of(first * capacity, group_slots), group_slots)
+        first, at = group_at(turn)
 
         @pl.loop(0, dp_count)
         def _(bin_index):
-            query = q_slots[bin_index, at, :]
-            scores = lax.dot_general(
-                query, k_slots[bin_index], NT, preferred_element_type=jnp.float32
+            query_marks = q_slots[bin_index, at, HEAD_DIM:]
+            sums = jnp.dot(
+                weights_buf[bin_index, at, :],
+                v_slots[bin_index],
+                preferred_element_type=jnp.float32,
             )
-            row_max = jnp.max(scores, axis=1, keepdims=True)
-            weights = jnp.exp2((scores - row_max) * exponent_scale).astype(jnp.bfloat16)
-            sums = jnp.dot(weights, v_slots[bin_index], preferred_element_type=jnp.float32)
             attended = (sums[:, :HEAD_DIM] / sums[:, HEAD_DIM:]).astype(jnp.bfloat16)
             factor = jnp.zeros((group_slots, HEAD_DIM), jnp.float32)
             for member in range(SEG_BIN):
-                mark = query[:, HEAD_DIM + member : HEAD_DIM + member + 1].astype(jnp.float32)
+                mark = query_marks[:, member : member + 1].astype(jnp.float32)
                 row = table_ref[pl.ds(bin_index * SEG_BIN + member, 1), :]
                 factor = jnp.where(mark == 0.0, 1.0 + row, factor)
             mixed = (attended.astype(jnp.float32) * factor).astype(jnp.bfloat16)
@@ -368,11 +405,11 @@
     count = dp_count * seq_count
     row_count, width = query_rows.shape
     capacity = 2 * row_count // dp_count
-    group = min(8, count)
+    group = count // 4
     me = lax.axis_index("dp") * seq_count + lax.axis_index("seq")
     head_weights = lax.dynamic_slice_in_dim(w_mod, me * HEAD_DIM, HEAD_DIM, 1)
     scale_table = scale_rows_table(timesteps, head_weights)
-    ids = jnp.broadcast_to(seg_ids[None, :], (8, row_count))
+    ids = seg_ids.reshape(1, row_count)
     vmem = pl.BlockSpec(memory_space=pltpu.VMEM)
     anywhere = pl.BlockSpec(memory_space=pl.ANY)
     slots = (dp_count, count * capacity, 2 * HEAD_DIM)
@@ -383,11 +420,12 @@
         out_specs=anywhere,
         scratch_shapes=[
             pltpu.VMEM((count, row_count, 3 * HEAD_DIM), jnp.bfloat16),
-            pltpu.VMEM((count, 8, row_count), jnp.int32),
+            pltpu.VMEM((count, 1, row_count), jnp.int32),
             pltpu.VMEM((count, dp_count * capacity, row_count), jnp.bfloat16),
             pltpu.VMEM(slots, jnp.bfloat16),
             pltpu.VMEM(slots, jnp.bfloat16),
             pltpu.VMEM(slots, jnp.bfloat16),
+            pltpu.VMEM((dp_count, count * capacity, count * capacity), jnp.bfloat16),
             pltpu.VMEM((dp_count, group * capacity, HEAD_DIM), jnp.bfloat16),
             pltpu.VMEM((count, row_count, HEAD_DIM), jnp.bfloat16),
             pltpu.SemaphoreType.DMA((4, count)),

time: 131 us -> 121 us (0.924)
  the two profiles are of different devices: /device:TPU:9 before, /device:TPU:15 now
where the time goes in v2:
time: 121 us
  Pallas kernels  116 us (96%)
  local copies, waits for them, and re-layouts  2.95 us (2%)
    pallas_call x1, Pallas kernels, head_shards(): pl.pallas_call(functools.partial(head_kernel, (dp_count, seq_count, capac...  116 us
    unnamed x3, local copies, waits for them, and re-layouts  2.95 us

profile of v2, /device:TPU:15, one launch (start us, length us, event | category | flops | bytes accessed | tf_op | source)
XLA Modules:
  0.0 120.7 jit_solution(15928354425162671221)
XLA Ops:
  0.0 0.0 copy-start
  0.0 0.8 convert_element_type.6
  0.8 0.1 multiply_cosine_fusion
  0.9 0.7 copy-done
  1.6 0.7 fusion.table_ref
  2.3 116.0 %shard_map.64 = bf16[128,4096]{1,0:T(8,128)(2,1)} custom-call(bf16[128,4096]{1,0:T(8,128)(2,1)} %q_ref.1, bf16[128,4096]{1,0:T(8,128)(2,1)} %k_ref.1, bf16[128,4096]{1,0:T(8,128)(2,1)} %v_ref.1, s32[1,128]{1,0:T(1,128)} %bitcast.1, f32[16,128]{1,0:T(8,128)} %fusion.table_ref), custom_call_target="tpu_custom_call" | custom-call | tf_op jit(solution)/shard_map/pallas_call | solution.py:416
  118.4 2.3 %copy.8 = bf16[128,4096]{1,0:T(8,128)(2,1)} copy(bf16[128,4096]{1,0:T(8,128)(2,1)} %shard_map.64) | data formatting | bytes 2097152
  (1 shorter events, 0.0 us)
Async XLA Ops:
  0.0 1.6 %copy-start = (bf16[256,4096]{1,0:T(8,128)(2,1)S(1)}, bf16[256,4096]{1,0:T(8,128)(2,1)}, u32[]{:S(2)}) copy-start(bf16[256,4096]{1,0:T(8,128)(2,1)} %param.11) | copy-start | bytes 6291460

commit v3 on v2

--- a/solution.py
+++ b/solution.py
@@ -138,7 +138,6 @@
     q_slots,
     k_slots,
     v_slots,
-    weights_buf,
     group_out,
     out_buf,
     sem_send,
@@ -151,7 +150,7 @@
     row_count = q_ref.shape[0]
     slot_count = dp_count * capacity
     me = lax.axis_index("dp") * seq_count + lax.axis_index("seq")
-    sources = (k_ref, q_ref, v_ref)
+    sources = (k_ref, v_ref, q_ref)
 
     def device_of(index):
         return (index // seq_count, index % seq_count)
@@ -231,14 +230,14 @@
     each_peer(greet)
     pl.semaphore_wait(barrier, count - 1)
 
-    def send_qk(away, shift):
+    def send_first(away, shift):
         target = peer(away, shift)
         ids_copy(target, me).start()
         part_copy(0, target, me).start()
-        part_copy(1, target, me).start()
-
-    each_peer(send_qk)
-    each_peer(lambda away, shift: part_copy(2, peer(away, shift), me).start())
+
+    each_peer(send_first)
+    for part in (1, 2):
+        each_peer(lambda away, shift: part_copy(part, peer(away, shift), me).start())
 
     v_slots[:, :, HEAD_DIM:] = jnp.ones(
         (dp_count, count * capacity, HEAD_DIM), jnp.bfloat16
@@ -249,9 +248,28 @@
     ).astype(jnp.bfloat16)
     part_lane = lax.broadcasted_iota(jnp.int32, (1, HEAD_DIM), 1) < SEG_BIN
 
-    def place_qk(origin, ids):
-        bins = ids // SEG_BIN
-        member = ids - bins * SEG_BIN
+    def member_hits(origin):
+        ids = ids_buf[origin]
+        member = ids - ids // SEG_BIN * SEG_BIN
+        return lax.broadcasted_iota(jnp.int32, (HEAD_DIM, row_count), 0) == member
+
+    def marks_of(place, hits):
+        return lax.dot_general(
+            place, hits.astype(jnp.bfloat16), NT, preferred_element_type=jnp.float32
+        )
+
+    def placed_part(place, origin, part):
+        rows = rows_buf[origin, :, part * HEAD_DIM : (part + 1) * HEAD_DIM]
+        return jnp.dot(place, rows, preferred_element_type=jnp.float32)
+
+    def by_bin(value):
+        return value.astype(jnp.bfloat16).reshape((dp_count, capacity, HEAD_DIM))
+
+    def slots_at(index):
+        return pl.ds(pl.multiple_of(index * capacity, capacity), capacity)
+
+    def place_k(origin):
+        bins = ids_buf[origin] // SEG_BIN
         bin_hits = lax.broadcasted_iota(jnp.int32, (16, row_count), 0) == bins
         ranks = jnp.dot(
             bin_hits.astype(jnp.bfloat16), before, preferred_element_type=jnp.float32
@@ -262,129 +280,106 @@
             lax.broadcasted_iota(jnp.int32, (slot_count, row_count), 0) == slot
         ).astype(jnp.bfloat16)
         place_buf[origin] = place
-        member_hits = (
-            lax.broadcasted_iota(jnp.int32, (HEAD_DIM, row_count), 0) == member
-        )
-        own_member = lax.dot_general(
-            place, member_hits.astype(jnp.bfloat16), NT, preferred_element_type=jnp.float32
-        )
-        other_member = lax.dot_general(
-            place,
-            jnp.logical_not(member_hits).astype(jnp.bfloat16),
-            NT,
-            preferred_element_type=jnp.float32,
-        )
+        other_member = marks_of(place, jnp.logical_not(member_hits(origin)))
+        k_marks = jnp.where(part_lane, 1.0 - other_member, 0.0)
+        k_slots[:, slots_at(origin), :HEAD_DIM] = by_bin(placed_part(place, origin, 0))
+        k_slots[:, slots_at(origin), HEAD_DIM:] = by_bin(k_marks)
+
+    def place_v(origin):
+        placed = placed_part(place_buf[origin], origin, 1)
+        v_slots[:, slots_at(origin), :HEAD_DIM] = by_bin(placed)
+
+    def place_q(origin, inner):
+        place = place_buf[origin]
+        own_member = marks_of(place, member_hits(origin))
         q_marks = jnp.where(part_lane, (own_member - 1.0) * EXCLUDED, 0.0)
-        k_marks = jnp.where(part_lane, 1.0 - other_member, 0.0)
-        placed = jnp.dot(
-            place, rows_buf[origin, :, : 2 * HEAD_DIM], preferred_element_type=jnp.float32
-        ).astype(jnp.bfloat16)
-        at = pl.ds(pl.multiple_of(origin * capacity, capacity), capacity)
-        shape = (dp_count, capacity, HEAD_DIM)
-        k_slots[:, at, :HEAD_DIM] = placed[:, :HEAD_DIM].reshape(shape)
-        q_slots[:, at, :HEAD_DIM] = placed[:, HEAD_DIM:].reshape(shape)
-        k_slots[:, at, HEAD_DIM:] = k_marks.astype(jnp.bfloat16).reshape(shape)
-        q_slots[:, at, HEAD_DIM:] = q_marks.astype(jnp.bfloat16).reshape(shape)
-
-    def place_v(origin):
-        placed = jnp.dot(
-            place_buf[origin],
-            rows_buf[origin, :, 2 * HEAD_DIM :],
-            preferred_element_type=jnp.float32,
-        ).astype(jnp.bfloat16)
-        at = pl.ds(pl.multiple_of(origin * capacity, capacity), capacity)
-        v_slots[:, at, :HEAD_DIM] = placed.reshape((dp_count, capacity, HEAD_DIM))
-
+        at = slice(inner * capacity, (inner + 1) * capacity)
+        q_slots[:, at, :HEAD_DIM] = by_bin(placed_part(place, origin, 2))
+        q_slots[:, at, HEAD_DIM:] = by_bin(q_marks)
+
+    ids_buf[me] = ids_ref[...]
     own_copy(0).wait()
-    own_copy(1).wait()
-    place_qk(me, ids_ref[...])
-
-    def take_qk(away, shift):
+    place_k(me)
+
+    def take_k(away, shift):
         origin = peer(away, -shift)
         ids_copy(me, origin).wait_recv()
         part_copy(0, me, origin).wait_recv()
+        place_k(origin)
+
+    each_peer(take_k)
+    own_copy(1).wait()
+    place_v(me)
+
+    def take_v(away, shift):
+        origin = peer(away, -shift)
         part_copy(1, me, origin).wait_recv()
-        place_qk(origin, ids_buf[origin])
-
-    each_peer(take_qk)
+        place_v(origin)
+
+    each_peer(take_v)
 
     exponent_scale = 1.0 / (math.sqrt(HEAD_DIM) * math.log(2.0))
     group_slots = group * capacity
-    groups = count // group
-
-    def group_at(turn):
-        first = ((me // group + groups // 2 + turn) % groups) * group
-        return first, pl.ds(pl.multiple_of(first * capacity, group_slots), group_slots)
-
-    @pl.loop(0, groups)
-    def _(turn):
-        _, at = group_at(turn)
-
-        @pl.loop(0, dp_count)
+
+    def attend_group(away, turn):
+        for inner in range(group):
+            shift = turn * group + inner
+            origin = peer(away, -shift)
+            if away == 0 and inner == 0:
+
+                @pl.when(turn == 0)
+                def _():
+                    own_copy(2).wait()
+
+                @pl.when(turn > 0)
+                def _():
+                    part_copy(2, me, origin).wait_recv()
+            else:
+                part_copy(2, me, origin).wait_recv()
+            place_q(origin, inner)
+
+        @pl.loop(0, dp_count, unroll=8)
         def _(bin_index):
+            query = q_slots[bin_index]
             scores = lax.dot_general(
-                q_slots[bin_index, at, :],
-                k_slots[bin_index],
-                NT,
-                preferred_element_type=jnp.float32,
+                query, k_slots[bin_index], NT, preferred_element_type=jnp.float32
             )
             row_max = jnp.max(scores, axis=1, keepdims=True)
-            weights_buf[bin_index, at, :] = jnp.exp2(
-                (scores - row_max) * exponent_scale
-            ).astype(jnp.bfloat16)
-
-    own_copy(2).wait()
-    place_v(me)
-
-    @pl.loop(1, half)
-    def _(shift):
-        origin = peer(0, -shift)
-        part_copy(2, me, origin).wait_recv()
-        place_v(origin)
-
-    @pl.loop(0, half)
-    def _(shift):
-        origin = peer(1, -shift)
-        part_copy(2, me, origin).wait_recv()
-        place_v(origin)
-
-    @pl.loop(0, groups)
-    def _(turn):
-        first, at = group_at(turn)
-
-        @pl.loop(0, dp_count)
-        def _(bin_index):
-            query_marks = q_slots[bin_index, at, HEAD_DIM:]
-            sums = jnp.dot(
-                weights_buf[bin_index, at, :],
-                v_slots[bin_index],
-                preferred_element_type=jnp.float32,
-            )
+            weights = jnp.exp2((scores - row_max) * exponent_scale).astype(jnp.bfloat16)
+            sums = jnp.dot(weights, v_slots[bin_index], preferred_element_type=jnp.float32)
             attended = (sums[:, :HEAD_DIM] / sums[:, HEAD_DIM:]).astype(jnp.bfloat16)
             factor = jnp.zeros((group_slots, HEAD_DIM), jnp.float32)
             for member in range(SEG_BIN):
-                mark = query_marks[:, member : member + 1].astype(jnp.float32)
+                mark = query[:, HEAD_DIM + member : HEAD_DIM + member + 1].astype(jnp.float32)
                 row = table_ref[pl.ds(bin_index * SEG_BIN + member, 1), :]
                 factor = jnp.where(mark == 0.0, 1.0 + row, factor)
             mixed = (attended.astype(jnp.float32) * factor).astype(jnp.bfloat16)
             group_out[bin_index] = mixed
 
         for inner in range(group):
-            target = first + inner
+            target = peer(away, -(turn * group + inner))
             slots = group_out[:, inner * capacity : (inner + 1) * capacity, :].reshape(
                 (slot_count, HEAD_DIM)
             )
             out_buf[target] = lax.dot_general(
                 place_buf[target], slots, TN, preferred_element_type=jnp.float32
             ).astype(jnp.bfloat16)
-
-            @pl.when(target != me)
-            def _():
+            if away == 0 and inner == 0:
+
+                @pl.when(turn == 0)
+                def _():
+                    own_out().start()
+
+                @pl.when(turn > 0)
+                def _():
+                    out_copy(target, me).start()
+            else:
                 out_copy(target, me).start()
 
-            @pl.when(target == me)
-            def _():
-                own_out().start()
+    @pl.loop(0, half // group)
+    def _(turn):
+        attend_group(0, turn)
+        attend_group(1, turn)
 
     @pl.loop(1, count)
     def _(step):
@@ -422,10 +417,9 @@
             pltpu.VMEM((count, row_count, 3 * HEAD_DIM), jnp.bfloat16),
             pltpu.VMEM((count, 1, row_count), jnp.int32),
             pltpu.VMEM((count, dp_count * capacity, row_count), jnp.bfloat16),
+            pltpu.VMEM((dp_count, group * capacity, 2 * HEAD_DIM), jnp.bfloat16),
             pltpu.VMEM(slots, jnp.bfloat16),
             pltpu.VMEM(slots, jnp.bfloat16),
-            pltpu.VMEM(slots, jnp.bfloat16),
-            pltpu.VMEM((dp_count, count * capacity, count * capacity), jnp.bfloat16),
             pltpu.VMEM((dp_count, group * capacity, HEAD_DIM), jnp.bfloat16),
             pltpu.VMEM((count, row_count, HEAD_DIM), jnp.bfloat16),
             pltpu.SemaphoreType.DMA((4, count)),

time: 121 us -> 110 us (0.909)
  the two profiles are of different devices: /device:TPU:15 before, /device:TPU:9 now
where the time goes in v3:
time: 110 us; the launch traced here: 109 us
  Pallas kernels  104 us (95%)
  local copies, waits for them, and re-layouts  2.95 us (3%)
    pallas_call x1, Pallas kernels, head_shards(): pl.pallas_call(functools.partial(head_kernel, (dp_count, seq_count, capac...  104 us
    unnamed x3, local copies, waits for them, and re-layouts  2.95 us

profile of v3, /device:TPU:9, one launch (start us, length us, event | category | flops | bytes accessed | tf_op | source)
XLA Modules:
  0.0 108.7 jit_solution(8567306624774171228)
XLA Ops:
  0.0 0.0 copy-start
  0.0 0.8 convert_element_type.6
  0.8 0.1 multiply_cosine_fusion
  0.9 0.7 copy-done
  1.6 0.7 fusion.table_ref
  2.3 104.1 %shard_map.64 = bf16[128,4096]{1,0:T(8,128)(2,1)} custom-call(bf16[128,4096]{1,0:T(8,128)(2,1)} %q_ref.1, bf16[128,4096]{1,0:T(8,128)(2,1)} %k_ref.1, bf16[128,4096]{1,0:T(8,128)(2,1)} %v_ref.1, s32[1,128]{1,0:T(1,128)} %bitcast.1, f32[16,128]{1,0:T(8,128)} %fusion.table_ref), custom_call_target="tpu_custom_call" | custom-call | tf_op jit(solution)/shard_map/pallas_call | solution.py:411
  106.4 2.3 %copy.8 = bf16[128,4096]{1,0:T(8,128)(2,1)} copy(bf16[128,4096]{1,0:T(8,128)(2,1)} %shard_map.64) | data formatting | bytes 2097152
  (1 shorter events, 0.0 us)
Async XLA Ops:
  0.0 1.6 %copy-start = (bf16[256,4096]{1,0:T(8,128)(2,1)S(1)}, bf16[256,4096]{1,0:T(8,128)(2,1)}, u32[]{:S(2)}) copy-start(bf16[256,4096]{1,0:T(8,128)(2,1)} %param.11) | copy-start | bytes 6291460

commit v4 on v3

--- a/solution.py
+++ b/solution.py
@@ -410,9 +410,9 @@
     slots = (dp_count, count * capacity, 2 * HEAD_DIM)
     return pl.pallas_call(
         functools.partial(head_kernel, (dp_count, seq_count, capacity, group)),
-        out_shape=jax.ShapeDtypeStruct((row_count, width), jnp.bfloat16),
+        out_shape=pltpu.VMEM((row_count, width), jnp.bfloat16),
         in_specs=[anywhere, anywhere, anywhere, vmem, vmem],
-        out_specs=anywhere,
+        out_specs=vmem,
         scratch_shapes=[
             pltpu.VMEM((count, row_count, 3 * HEAD_DIM), jnp.bfloat16),
             pltpu.VMEM((count, 1, row_count), jnp.int32),

time: 110 us -> 108 us (0.982)
  local copies, waits for them, and re-layouts: 2.95 us -> 1.64 us
    unnamed x3, local copies, waits for them, and re-layouts: 2.95 us -> 1.64 us
where the time goes in v4:
time: 108 us; the launch traced here: 107 us
  Pallas kernels  104 us (96%)
  local copies, waits for them, and re-layouts  1.64 us (2%)
    pallas_call x1, Pallas kernels, head_shards(): pl.pallas_call(functools.partial(head_kernel, (dp_count, seq_count, capac...  104 us

profile of v4, /device:TPU:9, one launch (start us, length us, event | category | flops | bytes accessed | tf_op | source)
XLA Modules:
  0.0 107.3 jit_solution(9191496236982428828)
XLA Ops:
  0.0 0.0 copy-start
  0.0 0.8 convert_element_type.6
  0.8 0.1 multiply_cosine_fusion
  0.9 0.7 copy-done
  1.6 0.7 fusion.table_ref
  2.3 103.9 %shard_map.64 = bf16[128,4096]{1,0:T(8,128)(2,1)S(1)} custom-call(bf16[128,4096]{1,0:T(8,128)(2,1)} %q_ref.1, bf16[128,4096]{1,0:T(8,128)(2,1)} %k_ref.1, bf16[128,4096]{1,0:T(8,128)(2,1)} %v_ref.1, s32[1,128]{1,0:T(1,128)} %bitcast.1, f32[16,128]{1,0:T(8,128)} %fusion.table_ref), custom_call_target="tpu_custom_call" | custom-call | tf_op jit(solution)/shard_map/pallas_call | solution.py:411
  106.3 1.0 copy.8
  (1 shorter events, 0.0 us)
Async XLA Ops:
  0.0 1.6 %copy-start = (bf16[256,4096]{1,0:T(8,128)(2,1)S(1)}, bf16[256,4096]{1,0:T(8,128)(2,1)}, u32[]{:S(2)}) copy-start(bf16[256,4096]{1,0:T(8,128)(2,1)} %param.11) | copy-start | bytes 6291460
